TPU v7x, 32 devices: a whole 2x2x4 slice. The times are simulated.
32 devices in a mesh: fsdp: 8 (over y, x, core), dp: 4 (over z).
Axes of the slice: x: 2, y: 2, z: 4, core: 2. Of those that a mesh axis runs over, the one named last changes fastest.
Arguments:
- tokens: bfloat16 [32768, 768], P(('fsdp', 'dp')), may hold values from -6 to 6
- crop_ids: int32 [32768], P(('fsdp', 'dp')), may hold values from 0 to 23, as said below
- gain_first: bfloat16 [768], P('fsdp'), may hold values from 0.25 to 1.75
- shift_first: bfloat16 [768], P('fsdp'), may hold values from -1 to 1
- joint_weight: bfloat16 [768, 2304], P('fsdp'), may hold values from -0.3125 to 0.3125
- joint_bias: bfloat16 [2, 768], P(None, 'fsdp'), may hold values from -1 to 1
- output_weight: bfloat16 [768, 768], P('fsdp'), may hold values from -0.4375 to 0.4375
- output_bias: bfloat16 [768], P('fsdp'), may hold values from -1 to 1
- gain_second: bfloat16 [768], P('fsdp'), may hold values from 0.25 to 1.75
- shift_second: bfloat16 [768], P('fsdp'), may hold values from -1 to 1
- up_weight: bfloat16 [768, 3072], P('fsdp'), may hold values from -0.21875 to 0.21875
- up_bias: bfloat16 [3072], P('fsdp'), may hold values from -1 to 1
- down_weight: bfloat16 [3072, 768], P('fsdp'), may hold values from -0.15625 to 0.15625
- down_bias: bfloat16 [768], P('fsdp'), may hold values from -1 to 1
- cotangent: bfloat16 [32768, 768], P(('fsdp', 'dp')), may hold values from -6 to 6
Outputs:
- activations: float32 [32768, 768], P(('fsdp', 'dp'))
- input_grad: float32 [32768, 768], P(('fsdp', 'dp'))
- grad_gain_first: float32 [768], P('fsdp')
- grad_shift_first: float32 [768], P('fsdp')
- grad_joint_weight: float32 [768, 2304], P('fsdp')
- grad_joint_bias: float32 [2, 768], P(None, 'fsdp')
- grad_output_weight: float32 [768, 768], P('fsdp')
- grad_output_bias: float32 [768], P('fsdp')
- grad_gain_second: float32 [768], P('fsdp')
- grad_shift_second: float32 [768], P('fsdp')
- grad_up_weight: float32 [768, 3072], P('fsdp')
- grad_up_bias: float32 [3072], P('fsdp')
- grad_down_weight: float32 [3072, 768], P('fsdp')
- grad_down_bias: float32 [768], P('fsdp')
Inputs may be any that keep to these rules, and one draw needn't show every extreme that they name: `crop_ids`: each device's 1024 tokens hold whole crops in random order: at least one global crop of 197 tokens, local crops of 37 tokens, and at most one shorter remainder crop; the first device's block holds exactly one global crop. Ids number the crops of a block from 0 in order of position; a crop has at most 197 tokens and every block has a crop of exactly 197.
All inputs are finite; a program needn't handle non-finite values.
Results may differ from a plain program's by a relative error of at most 0.015.
Values may be sent and summed in bfloat16 or wider, within the bound.
No kernel may reach another device: no remote copies, remote signals or barrier semaphores. Data moves between devices by JAX's collectives and lax.ppermute only.
A program may use at most 256 MiB of HBM per device.

v0:
```python
import jax
import jax.numpy as jnp
from jax import lax
from jax.sharding import PartitionSpec as P

HD = 64


def layer_norm(values, gain, shift):
    center = values - jnp.mean(values, axis=-1, keepdims=True)
    spread = jnp.mean(center * center, axis=-1, keepdims=True)
    return center * lax.rsqrt(spread + 1e-06) * gain + shift


def exact_gelu(values):
    return jax.nn.gelu(values, approximate=False)


def on_device(
    tokens,
    crop_ids,
    gain_first,
    shift_first,
    joint_weight,
    joint_bias,
    output_weight,
    output_bias,
    gain_second,
    shift_second,
    up_weight,
    up_bias,
    down_weight,
    down_bias,
    cotangent,
):
    row_count = tokens.shape[0]
    model_width = tokens.shape[1]
    head_count = model_width // HD
    score_scale = HD ** (-0.5)
    block_rows = min(512, row_count)
    block_count = row_count // block_rows
    attn_full = (
        lax.all_gather(gain_first, "fsdp", axis=0, tiled=True),
        lax.all_gather(shift_first, "fsdp", axis=0, tiled=True),
        lax.all_gather(joint_weight, "fsdp", axis=0, tiled=True),
        lax.all_gather(joint_bias, "fsdp", axis=1, tiled=True),
        lax.all_gather(output_weight, "fsdp", axis=0, tiled=True),
        lax.all_gather(output_bias, "fsdp", axis=0, tiled=True),
    )
    gain_one, shift_one, joint_full, joint_bias_full, output_full, output_bias_full = attn_full
    inputs = tokens.astype(jnp.float32)
    normed_first, pull_first = jax.vjp(
        layer_norm, inputs, gain_one.astype(jnp.float32), shift_one.astype(jnp.float32)
    )
    hidden_first = normed_first.astype(jnp.bfloat16)
    bias_joint = joint_bias_full.astype(jnp.float32)
    bias_row = jnp.concatenate(
        [bias_joint[0], jnp.zeros((model_width,), jnp.float32), bias_joint[1]]
    )
    joint_proj = (
        jnp.dot(hidden_first, joint_full, preferred_element_type=jnp.float32) + bias_row
    ).astype(jnp.bfloat16)
    queries = joint_proj[:, :model_width].reshape(row_count, head_count, HD)
    key_rows = joint_proj[:, model_width : 2 * model_width].reshape(row_count, head_count, HD)
    value_rows = joint_proj[:, 2 * model_width :].reshape(row_count, head_count, HD)
    query_blocks = queries.reshape(block_count, block_rows, head_count, HD)
    crop_blocks = crop_ids.reshape(block_count, block_rows)

    def masked_scores(query_block, crop_block):
        scores = (
            jnp.einsum("qhd,khd->hqk", query_block, key_rows, preferred_element_type=jnp.float32)
            * score_scale
        )
        same_crop = crop_block[:, None] == crop_ids[None, :]
        return jnp.where(same_crop[None], scores, -1e30)

    def attend(inputs_block):
        query_block, crop_block = inputs_block
        scores = masked_scores(query_block, crop_block)
        top_score = jnp.max(scores, axis=-1, keepdims=True)
        expo = jnp.exp(scores - top_score)
        total = jnp.sum(expo, axis=-1, keepdims=True)
        weights_low = (expo / total).astype(jnp.bfloat16)
        mixed_block = jnp.einsum(
            "hqk,khd->qhd", weights_low, value_rows, preferred_element_type=jnp.float32
        )
        log_total = top_score[..., 0] + jnp.log(total[..., 0])
        return (mixed_block.astype(jnp.bfloat16), log_total)

    mixed_blocks, log_totals = lax.map(attend, (query_blocks, crop_blocks))
    mixed_heads = mixed_blocks.reshape(row_count, model_width)
    branch_first = jnp.dot(
        mixed_heads, output_full, preferred_element_type=jnp.float32
    ) + output_bias_full.astype(jnp.float32)
    middle = inputs + branch_first
    mlp_full = (
        lax.all_gather(gain_second, "fsdp", axis=0, tiled=True),
        lax.all_gather(shift_second, "fsdp", axis=0, tiled=True),
        lax.all_gather(up_weight, "fsdp", axis=0, tiled=True),
        lax.all_gather(up_bias, "fsdp", axis=0, tiled=True),
        lax.all_gather(down_weight, "fsdp", axis=0, tiled=True),
        lax.all_gather(down_bias, "fsdp", axis=0, tiled=True),
    )
    gain_two, shift_two, up_full, up_bias_full, down_full, down_bias_full = mlp_full
    normed_second, pull_second = jax.vjp(
        layer_norm, middle, gain_two.astype(jnp.float32), shift_two.astype(jnp.float32)
    )
    hidden_second = normed_second.astype(jnp.bfloat16)
    up_value = jnp.dot(
        hidden_second, up_full, preferred_element_type=jnp.float32
    ) + up_bias_full.astype(jnp.float32)
    active_value, pull_gelu = jax.vjp(exact_gelu, up_value)
    active = active_value.astype(jnp.bfloat16)
    activations = (
        middle
        + jnp.dot(active, down_full, preferred_element_type=jnp.float32)
        + down_bias_full.astype(jnp.float32)
    )
    mlp_back = (
        lax.all_gather(gain_second, "fsdp", axis=0, tiled=True),
        lax.all_gather(shift_second, "fsdp", axis=0, tiled=True),
        lax.all_gather(up_weight, "fsdp", axis=0, tiled=True),
        lax.all_gather(up_bias, "fsdp", axis=0, tiled=True),
        lax.all_gather(down_weight, "fsdp", axis=0, tiled=True),
        lax.all_gather(down_bias, "fsdp", axis=0, tiled=True),
    )
    up_back = mlp_back[2]
    down_back = mlp_back[4]
    grad_out = cotangent.astype(jnp.float32)
    grad_down_bias = jnp.sum(grad_out, axis=0)
    grad_down_weight = jnp.einsum(
        "tf,td->fd", active, cotangent, preferred_element_type=jnp.float32
    )
    grad_active = jnp.einsum("td,fd->tf", cotangent, down_back, preferred_element_type=jnp.float32)
    (grad_up_value,) = pull_gelu(grad_active)
    grad_up_low = grad_up_value.astype(jnp.bfloat16)
    grad_up_bias = jnp.sum(grad_up_low.astype(jnp.float32), axis=0)
    grad_up_weight = jnp.einsum(
        "td,tf->df", hidden_second, grad_up_low, preferred_element_type=jnp.float32
    )
    grad_hidden_second = jnp.einsum(
        "tf,df->td", grad_up_low, up_back, preferred_element_type=jnp.float32
    )
    grad_middle, grad_gain_second, grad_shift_second = pull_second(grad_hidden_second)
    grad_middle = grad_middle + grad_out
    mlp_terms = (
        grad_gain_second,
        grad_shift_second,
        grad_up_weight,
        grad_up_bias,
        grad_down_weight,
        grad_down_bias,
    )
    mlp_sums = (
        lax.psum_scatter(mlp_terms[0], "fsdp", scatter_dimension=0, tiled=True),
        lax.psum_scatter(mlp_terms[1], "fsdp", scatter_dimension=0, tiled=True),
        lax.psum_scatter(mlp_terms[2], "fsdp", scatter_dimension=0, tiled=True),
        lax.psum_scatter(mlp_terms[3], "fsdp", scatter_dimension=0, tiled=True),
        lax.psum_scatter(mlp_terms[4], "fsdp", scatter_dimension=0, tiled=True),
        lax.psum_scatter(mlp_terms[5], "fsdp", scatter_dimension=0, tiled=True),
    )
    attn_back = (
        lax.all_gather(gain_first, "fsdp", axis=0, tiled=True),
        lax.all_gather(shift_first, "fsdp", axis=0, tiled=True),
        lax.all_gather(joint_weight, "fsdp", axis=0, tiled=True),
        lax.all_gather(joint_bias, "fsdp", axis=1, tiled=True),
        lax.all_gather(output_weight, "fsdp", axis=0, tiled=True),
        lax.all_gather(output_bias, "fsdp", axis=0, tiled=True),
    )
    joint_back = attn_back[2]
    output_back = attn_back[4]
    grad_branch = grad_middle.astype(jnp.bfloat16)
    grad_output_bias = jnp.sum(grad_branch.astype(jnp.float32), axis=0)
    grad_output_weight = jnp.einsum(
        "td,te->de", mixed_heads, grad_branch, preferred_element_type=jnp.float32
    )
    grad_mixed = jnp.einsum(
        "te,de->td", grad_branch, output_back, preferred_element_type=jnp.float32
    ).astype(jnp.bfloat16)
    grad_mixed_blocks = grad_mixed.reshape(block_count, block_rows, head_count, HD)

    def attend_back(carry, inputs_block):
        grad_key_sum, grad_value_sum = carry
        query_block, crop_block, log_total, grad_block = inputs_block
        scores = masked_scores(query_block, crop_block)
        weights = jnp.exp(scores - log_total[..., None])
        weights_low = weights.astype(jnp.bfloat16)
        grad_value_sum = grad_value_sum + jnp.einsum(
            "hqk,qhd->khd", weights_low, grad_block, preferred_element_type=jnp.float32
        )
        grad_weights = jnp.einsum(
            "qhd,khd->hqk", grad_block, value_rows, preferred_element_type=jnp.float32
        )
        inner = jnp.sum(weights * grad_weights, axis=-1, keepdims=True)
        grad_scores = (weights * (grad_weights - inner)).astype(jnp.bfloat16)
        grad_query = (
            jnp.einsum("hqk,khd->qhd", grad_scores, key_rows, preferred_element_type=jnp.float32)
            * score_scale
        )
        grad_key_sum = (
            grad_key_sum
            + jnp.einsum(
                "hqk,qhd->khd", grad_scores, query_block, preferred_element_type=jnp.float32
            )
            * score_scale
        )
        return ((grad_key_sum, grad_value_sum), grad_query)

    empty_heads = jnp.zeros((row_count, head_count, HD), jnp.float32)
    (grad_keys, grad_values), grad_query_blocks = lax.scan(
        attend_back,
        (empty_heads, empty_heads),
        (query_blocks, crop_blocks, log_totals, grad_mixed_blocks),
    )
    grad_joint = jnp.concatenate(
        [
            grad_query_blocks.reshape(row_count, model_width),
            grad_keys.reshape(row_count, model_width),
            grad_values.reshape(row_count, model_width),
        ],
        axis=1,
    ).astype(jnp.bfloat16)
    grad_joint_wide = grad_joint.astype(jnp.float32)
    grad_joint_bias = jnp.stack(
        [
            jnp.sum(grad_joint_wide[:, :model_width], axis=0),
            jnp.sum(grad_joint_wide[:, 2 * model_width :], axis=0),
        ]
    )
    grad_joint_weight = jnp.einsum(
        "td,te->de", hidden_first, grad_joint, preferred_element_type=jnp.float32
    )
    grad_hidden_first = jnp.einsum(
        "te,de->td", grad_joint, joint_back, preferred_element_type=jnp.float32
    )
    grad_inputs, grad_gain_first, grad_shift_first = pull_first(grad_hidden_first)
    input_grad = grad_inputs + grad_middle
    attn_terms = (
        grad_gain_first,
        grad_shift_first,
        grad_joint_weight,
        grad_joint_bias,
        grad_output_weight,
        grad_output_bias,
    )
    attn_sums = (
        lax.psum_scatter(attn_terms[0], "fsdp", scatter_dimension=0, tiled=True),
        lax.psum_scatter(attn_terms[1], "fsdp", scatter_dimension=0, tiled=True),
        lax.psum_scatter(attn_terms[2], "fsdp", scatter_dimension=0, tiled=True),
        lax.psum_scatter(attn_terms[3], "fsdp", scatter_dimension=1, tiled=True),
        lax.psum_scatter(attn_terms[4], "fsdp", scatter_dimension=0, tiled=True),
        lax.psum_scatter(attn_terms[5], "fsdp", scatter_dimension=0, tiled=True),
    )
    totals = (
        lax.psum(attn_sums[0].astype(jnp.bfloat16), "dp").astype(jnp.float32),
        lax.psum(attn_sums[1].astype(jnp.bfloat16), "dp").astype(jnp.float32),
        lax.psum(attn_sums[2].astype(jnp.bfloat16), "dp").astype(jnp.float32),
        lax.psum(attn_sums[3].astype(jnp.bfloat16), "dp").astype(jnp.float32),
        lax.psum(attn_sums[4].astype(jnp.bfloat16), "dp").astype(jnp.float32),
        lax.psum(attn_sums[5].astype(jnp.bfloat16), "dp").astype(jnp.float32),
        lax.psum(mlp_sums[0].astype(jnp.bfloat16), "dp").astype(jnp.float32),
        lax.psum(mlp_sums[1].astype(jnp.bfloat16), "dp").astype(jnp.float32),
        lax.psum(mlp_sums[2].astype(jnp.bfloat16), "dp").astype(jnp.float32),
        lax.psum(mlp_sums[3].astype(jnp.bfloat16), "dp").astype(jnp.float32),
        lax.psum(mlp_sums[4].astype(jnp.bfloat16), "dp").astype(jnp.float32),
        lax.psum(mlp_sums[5].astype(jnp.bfloat16), "dp").astype(jnp.float32),
    )
    return (
        activations,
        input_grad,
        totals[0],
        totals[1],
        totals[2],
        totals[3],
        totals[4],
        totals[5],
        totals[6],
        totals[7],
        totals[8],
        totals[9],
        totals[10],
        totals[11],
    )


def solution(mesh):
    placed = (
        P(("fsdp", "dp"), None),
        P(("fsdp", "dp")),
        P("fsdp"),
        P("fsdp"),
        P("fsdp", None),
        P(None, "fsdp"),
        P("fsdp", None),
        P("fsdp"),
        P("fsdp"),
        P("fsdp"),
        P("fsdp", None),
        P("fsdp"),
        P("fsdp", None),
        P("fsdp"),
        P(("fsdp", "dp"), None),
    )
    return jax.shard_map(
        on_device,
        mesh=mesh,
        in_specs=placed,
        out_specs=(
            P(("fsdp", "dp"), None),
            P(("fsdp", "dp"), None),
            P("fsdp"),
            P("fsdp"),
            P("fsdp", None),
            P(None, "fsdp"),
            P("fsdp", None),
            P("fsdp"),
            P("fsdp"),
            P("fsdp"),
            P("fsdp", None),
            P("fsdp"),
            P("fsdp", None),
            P("fsdp"),
        ),
        check_vma=False,
    )
```

profile of v0, /device:TPU:0, one launch (start us, length us, event | category | flops | bytes accessed | tf_op | source)
XLA Modules:
  0.0 798.5 jit_solution(4974741141929564460)
XLA Ops:
  17.8 26.7 %all-reduce.14 = (bf16[768]{0:T(1024)(128)(2,1)S(1)}, bf16[768]{0:T(1024)(128)(2,1)S(1)}, bf16[768]{0:T(1024)(128)(2,1)S(1)}, bf16[768]{0:T(1024)(128)(2,1)S(1)}...) all-reduce(bf16[768]{0:T(1024)(128)(2,1)S(1)} %dynamic-update-slice., ...), channel_id=1, replica_groups=mesh['fsdp'=8,'dp'=4] {'fsdp'}, use_global_device_ids=true, to_apply=%add.1 | all-reduce | flops 4608 | bytes 18432
  87.9 72.2 %while.27 = (s32[]{:T(128)}, bf16[2,512,12,64]{1,3,2,0:T(8,128)(2,1)}, f32[2,12,512]{2,1,0:T(8,128)S(1)}, s32[2,512]{1,0:T(2,128)S(1)}, s32[1024]{0:T(1024)S(1)}...) while((s32[]{:T(128)}, ...), condition=%wide.region_5.6_spmd, body=%wide.region_2.5_spmd.sunk | while | flops 1687021568 | bytes 189499568 | solution.py:90
  88.3 11.1 %fusion.114 = (f32[12,512]{1,0:T(8,128)S(1)}, f32[12,512,1024]{2,1,0:T(8,128)}) fusion(pred[512,1024]{1,0:T(8,128)(4,1)S(1)} %broadcast_compare_fusion.4, bf16[1024,12,64]{0,2,1:T(8,128)(2,1)S(1)} %get-tuple-element.534, bf16[2,512,12,64]{1,3,2,0:T(8,128)(2,1)S(1)} %get-tuple-element.533, s32[]{:T(128)S(6)} %copy.120), kind=kOutput, calls=%fused_computation.3.clone.1 | convolution fusion | flops 824174592 | bytes 28073988 | tf_op jit(solution)/shard_map/while/body/eval_jaxpr/qhd,khd->hqk/dot_general | solution.py:71
  99.4 12.5 %fusion.115 = f32[12,512]{1,0:T(8,128)S(1)} fusion(f32[12,512,1024]{2,1,0:T(8,128)} %get-tuple-element.495, f32[12,512]{1,0:T(8,128)S(1)} %get-tuple-element.496, pred[512,1024]{1,0:T(8,128)(4,1)S(1)} %broadcast_compare_fusion.4), kind=kLoop, calls=%fused_computation.4.clone.1 | loop fusion | flops 25159680 | bytes 25739264 | tf_op jit(solution)/shard_map/while/body/eval_jaxpr/reduce_sum | solution.py:82
  124.1 10.7 %fusion.114 = (f32[12,512]{1,0:T(8,128)S(1)}, f32[12,512,1024]{2,1,0:T(8,128)}) fusion(pred[512,1024]{1,0:T(8,128)(4,1)S(1)} %broadcast_compare_fusion.4, bf16[1024,12,64]{0,2,1:T(8,128)(2,1)S(1)} %get-tuple-element.534, bf16[2,512,12,64]{1,3,2,0:T(8,128)(2,1)S(1)} %get-tuple-element.533, s32[]{:T(128)S(6)} %copy.120), kind=kOutput, calls=%fused_computation.3.clone.1 | convolution fusion | flops 824174592 | bytes 28073988 | tf_op jit(solution)/shard_map/while/body/eval_jaxpr/qhd,khd->hqk/dot_general | solution.py:71
  134.8 13.2 %fusion.115 = f32[12,512]{1,0:T(8,128)S(1)} fusion(f32[12,512,1024]{2,1,0:T(8,128)} %get-tuple-element.495, f32[12,512]{1,0:T(8,128)S(1)} %get-tuple-element.496, pred[512,1024]{1,0:T(8,128)(4,1)S(1)} %broadcast_compare_fusion.4), kind=kLoop, calls=%fused_computation.4.clone.1 | loop fusion | flops 25159680 | bytes 25739264 | tf_op jit(solution)/shard_map/while/body/eval_jaxpr/reduce_sum | solution.py:82
  170.6 37.9 %multiply_convert_fusion.1 = (bf16[1024,3072]{1,0:T(8,128)(2,1)}, f32[1024,3072]{1,0:T(8,128)}, f32[1024,3072]{1,0:T(8,128)}) fusion(f32[3072]{0:T(1024)S(1)} %bitcast.151, bf16[768,3072]{1,0:T(8,128)(2,1)} %all-gather.11.cloned.1.call-done, f32[1024,768]{0,1:T(8,128)S(1)} %get-tuple-element.378, f32[768]{0:T(1024)S(1)} %copy-done.51, ...), kind=kOutput, calls=%fused_computation.50 | convolution fusion | flops 5043388416 | bytes 39348224 | tf_op jit(solution)/shard_map/dot_general | solution.py:109
  208.5 18.9 %convert_reduce_fusion = (f32[3072]{0:T(1024)}, bf16[1024,3072]{1,0:T(8,128)(2,1)}) fusion(f32[1024,3072]{1,0:T(8,128)} %get-tuple-element.365, bf16[1024,768]{1,0:T(8,128)(2,1)} %param.33, bf16[3072,768]{1,0:T(8,128)(2,1)} %all-gather.13.cloned.1.call-done, f32[1024,3072]{1,0:T(8,128)} %get-tuple-element.379, f32[3072]{0:T(1024)S(1)} %bitcast.152), kind=kOutput, calls=%fused_computation.48 | convolution fusion | flops 4885312512 | bytes 37773312 | tf_op jit(solution)/shard_map/td,fd->tf/dot_general | solution.py:134
  257.4 169.1 %while.28 = (s32[]{:T(128)}, f32[1024,12,64]{0,2,1:T(8,128)}, f32[1024,12,64]{0,2,1:T(8,128)}, bf16[2,512,12,64]{1,3,2,0:T(8,128)(2,1)}, bf16[2,512,12,64]{1,3,2...) while((s32[]{:T(128)}, f32[1024,12,64]{0,2,1:T(8,128)}, ...), condition=%wide.region_12.13_spmd.clone, body=%wide.region_10.12_spmd.clone.sunk | while | flops 4125747200 | bytes 225634512 | solution.py:210
  258.3 12.3 %fusion.126 = f32[12,512,1024]{2,1,0:T(8,128)} fusion(bf16[1024,12,64]{0,2,1:T(8,128)(2,1)S(1)} %get-tuple-element.570, bf16[2,512,12,64]{1,3,2,0:T(8,128)(2,1)} %get-tuple-element.567, s32[]{:T(128)S(6)} %copy.130), kind=kOutput, calls=%fused_computation.32.clone.1 | convolution fusion | flops 805306368 | bytes 27525124 | tf_op jit(solution)/shard_map/while/body/eval_jaxpr/qhd,khd->hqk/dot_general | solution.py:71
  270.5 13.5 %bitcast_add_fusion.5 = f32[1024,12,64]{0,2,1:T(8,128)} fusion(f32[1024,12,64]{0,2,1:T(8,128)} %get-tuple-element.552, f32[12,512,1024]{2,1,0:T(8,128)} %fusion.126, f32[12,512]{1,0:T(8,128)S(1)} %dynamic-slice_bitcast_fusion.2, pred[512,1024]{1,0:T(8,128)(4,1)S(1)} %broadcast_compare_fusion.5, pred[]{:T(512)S(6)} %compare.3, ...), kind=kOutput, calls=%fused_computation.24.clone.1 | convolution fusion | flops 832045056 | bytes 32800772 | tf_op jit(solution)/shard_map/while/body/eval_jaxpr/hqk,qhd->khd/dot_general | solution.py:188
  284.0 18.3 %multiply_reduce_fusion.5 = (f32[12,512]{1,0:T(8,128)S(1)}, f32[12,512,1024]{2,1,0:T(8,128)}) fusion(f32[12,512,1024]{2,1,0:T(8,128)} %fusion.126, f32[12,512]{1,0:T(8,128)S(1)} %dynamic-slice_bitcast_fusion.2, pred[512,1024]{1,0:T(8,128)(4,1)S(1)} %broadcast_compare_fusion.5, bf16[1024,12,64]{0,2,1:T(8,128)(2,1)} %get-tuple-element.573, ...), kind=kOutput, calls=%fused_computation.19.clone.1 | convolution fusion | flops 836757504 | bytes 53264388 | tf_op jit(solution)/shard_map/while/body/eval_jaxpr/qhd,khd->hqk/dot_general | solution.py:191
  302.3 21.3 %multiply_convert_fusion.3 = bf16[12,512,1024]{2,1,0:T(8,128)(2,1)} fusion(f32[12,512,1024]{2,1,0:T(8,128)} %get-tuple-element.508, f32[12,512,1024]{2,1,0:T(8,128)} %fusion.126, f32[12,512]{1,0:T(8,128)S(1)} %get-tuple-element.509, f32[12,512]{1,0:T(8,128)S(1)} %dynamic-slice_bitcast_fusion.2, pred[512,1024]{1,0:T(8,128)(4,1)S(1)} %broadcast_compare_fusion.5), kind=kLoop, calls=%fused_computation.18.clone.1 | loop fusion | flops 37748736 | bytes 63488000 | tf_op jit(solution)/shard_map/while/body/eval_jaxpr/convert_element_type | solution.py:195
  342.1 11.4 %fusion.126 = f32[12,512,1024]{2,1,0:T(8,128)} fusion(bf16[1024,12,64]{0,2,1:T(8,128)(2,1)S(1)} %get-tuple-element.570, bf16[2,512,12,64]{1,3,2,0:T(8,128)(2,1)} %get-tuple-element.567, s32[]{:T(128)S(6)} %copy.130), kind=kOutput, calls=%fused_computation.32.clone.1 | convolution fusion | flops 805306368 | bytes 27525124 | tf_op jit(solution)/shard_map/while/body/eval_jaxpr/qhd,khd->hqk/dot_general | solution.py:71
  353.5 14.4 %bitcast_add_fusion.5 = f32[1024,12,64]{0,2,1:T(8,128)} fusion(f32[1024,12,64]{0,2,1:T(8,128)} %get-tuple-element.552, f32[12,512,1024]{2,1,0:T(8,128)} %fusion.126, f32[12,512]{1,0:T(8,128)S(1)} %dynamic-slice_bitcast_fusion.2, pred[512,1024]{1,0:T(8,128)(4,1)S(1)} %broadcast_compare_fusion.5, pred[]{:T(512)S(6)} %compare.3, ...), kind=kOutput, calls=%fused_computation.24.clone.1 | convolution fusion | flops 832045056 | bytes 32800772 | tf_op jit(solution)/shard_map/while/body/eval_jaxpr/hqk,qhd->khd/dot_general | solution.py:188
  367.9 18.1 %multiply_reduce_fusion.5 = (f32[12,512]{1,0:T(8,128)S(1)}, f32[12,512,1024]{2,1,0:T(8,128)}) fusion(f32[12,512,1024]{2,1,0:T(8,128)} %fusion.126, f32[12,512]{1,0:T(8,128)S(1)} %dynamic-slice_bitcast_fusion.2, pred[512,1024]{1,0:T(8,128)(4,1)S(1)} %broadcast_compare_fusion.5, bf16[1024,12,64]{0,2,1:T(8,128)(2,1)} %get-tuple-element.573, ...), kind=kOutput, calls=%fused_computation.19.clone.1 | convolution fusion | flops 836757504 | bytes 53264388 | tf_op jit(solution)/shard_map/while/body/eval_jaxpr/qhd,khd->hqk/dot_general | solution.py:191
  386.0 21.3 %multiply_convert_fusion.3 = bf16[12,512,1024]{2,1,0:T(8,128)(2,1)} fusion(f32[12,512,1024]{2,1,0:T(8,128)} %get-tuple-element.508, f32[12,512,1024]{2,1,0:T(8,128)} %fusion.126, f32[12,512]{1,0:T(8,128)S(1)} %get-tuple-element.509, f32[12,512]{1,0:T(8,128)S(1)} %dynamic-slice_bitcast_fusion.2, pred[512,1024]{1,0:T(8,128)(4,1)S(1)} %broadcast_compare_fusion.5), kind=kLoop, calls=%fused_computation.18.clone.1 | loop fusion | flops 37748736 | bytes 63488000 | tf_op jit(solution)/shard_map/while/body/eval_jaxpr/convert_element_type | solution.py:195
  442.1 10.8 %fusion.60 = f32[768,3072]{1,0:T(8,128)} fusion(bf16[1024,3072]{1,0:T(8,128)(2,1)} %get-tuple-element.385, f32[1024,768]{0,1:T(8,128)} %copy-done.12, f32[768]{0:T(1024)S(1)} %copy-done.52, f32[768]{0:T(1024)S(1)} %copy-done.43, f32[1024]{0:T(1024)S(1)} %copy-done.45, f32[1024]{0:T(1024)S(1)} %copy-done.35), kind=kOutput, calls=%fused_computation.121 | convolution fusion | flops 4835770368 | bytes 18888704 | tf_op jit(solution)/shard_map/td,tf->df/dot_general | solution.py:138
  494.5 12.8 %reduce-scatter.8.cloned.1.call-done = f32[96,2304]{1,0:T(8,128)} async-done(((f32[768,2304]{1,0:T(8,128)}), f32[96,2304]{1,0:T(8,128)}) %reduce-scatter.8.cloned.1.call-update) | async-done | bytes 884752 | tf_op jit(solution)/shard_map/reduce_scatter | solution.py:249
  509.3 78.4 %reduce-scatter.12.cloned.1.call-done = f32[96,3072]{1,0:T(8,128)} async-done(((f32[768,3072]{1,0:T(8,128)}), f32[96,3072]{1,0:T(8,128)}) %reduce-scatter.12.cloned.1.call-update) | async-done | bytes 1179664 | tf_op jit(solution)/shard_map/reduce_scatter | solution.py:157
  589.9 78.2 %reduce-scatter.14.cloned.1.call-done = f32[384,768]{1,0:T(8,128)} async-done(((f32[3072,768]{1,0:T(8,128)}), f32[384,768]{1,0:T(8,128)}) %reduce-scatter.14.cloned.1.call-update) | async-done | bytes 1179664 | tf_op jit(solution)/shard_map/reduce_scatter | solution.py:159
  678.5 23.3 %all-reduce.13 = (bf16[768]{0:T(1024)(128)(2,1)S(1)}, bf16[768]{0:T(1024)(128)(2,1)S(1)}, bf16[768]{0:T(1024)(128)(2,1)S(1)}, bf16[768]{0:T(1024)(128)(2,1)S(1)}...) all-reduce(f32[768]{0:T(1024)S(1)} %get-tuple-element.293, ...), channel_id=2, replica_groups=mesh['fsdp'=8,'dp'=4] {'fsdp'}, use_global_device_ids=true, to_apply=%region_16.17.clone | all-reduce | flops 7680 | bytes 46080
  706.7 11.9 %all-reduce.15 = (bf16[96]{0:T(256)(128)(2,1)S(1)}, bf16[96]{0:T(256)(128)(2,1)S(1)}, bf16[2,96]{1,0:T(2,128)(2,1)S(1)}, bf16[96]{0:T(256)(128)(2,1)S(1)}, bf16[...) all-reduce(bf16[96]{0:T(256)(128)(2,1)S(1)} %dynamic-slice.33, ...), channel_id=1, replica_groups=mesh['fsdp'=8,'dp'=4] {'dp'}, use_global_device_ids=true, to_apply=%region_17.18 | all-reduce | flops 1152 | bytes 4608 | tf_op jit(solution)/shard_map/psum | solution.py:255
  722.9 61.4 %all-reduce.19.cloned.1.call-done = (bf16[96,2304]{1,0:T(8,128)(2,1)}, bf16[96,768]{1,0:T(8,128)(2,1)}, bf16[96,3072]{1,0:T(8,128)(2,1)}, bf16[384,768]{1,0:T(8,128)(2,1)}) async-done(((bf16[96,2304]{1,0:T(8,128)(2,1)}, bf16[96,768]{1,0:T(8,128)(2,1)}, bf16[96,3072]{1,0:T(8,128)(2,1)}, bf16[384,768]{1,0:T(8,128)(2,1)}), (bf16[96,2304]{1,0:T(8,128)(2,1)}, bf16[96,768]{1,0:T(8,128)(2,1)}, ...) | async-done | bytes 1769488 | tf_op jit(solution)/shard_map/psum | solution.py:257
  (279 shorter events, 241.9 us)
Async XLA Ops:
  7.2 62.2 %all-gather.7.cloned.1.call-start = ((), (), s32[]{:S(2)}) async-start(), calls=%async_computation.5 | async-start | bytes 3981312 | tf_op jit(solution)/shard_map/all_gather | solution.py:45
  7.9 158.0 %all-gather.9.cloned.1.call-start = ((), (), s32[]{:S(2)}) async-start(), calls=%async_computation.6 | async-start | bytes 1327104 | tf_op jit(solution)/shard_map/all_gather | solution.py:47
  8.7 161.6 %all-gather.11.cloned.1.call-start = ((), (), s32[]{:S(2)}) async-start(), calls=%async_computation.7 | async-start | bytes 5308416 | tf_op jit(solution)/shard_map/all_gather | solution.py:99
  9.4 199.1 %all-gather.13.cloned.1.call-start = ((), (), s32[]{:S(2)}) async-start(), calls=%async_computation.8 | async-start | bytes 5308416 | tf_op jit(solution)/shard_map/all_gather | solution.py:101
  10.0 482.9 %reduce-scatter.10.cloned.1.call-start = ((), (), s32[]{:S(2)}) async-start(), calls=%async_computation.10 | async-start | bytes 2654208 | tf_op jit(solution)/shard_map/reduce_scatter | solution.py:251
  44.5 24.9 %copy-start.53 = (f32[768]{0:T(1024)}, f32[768]{0:T(1024)S(1)}, u32[]{:S(2)}) copy-start(f32[768]{0:T(1024)S(1)} %convert_element_type.150) | copy-start | bytes 9220
  44.5 24.9 %copy-start.32 = (f32[768]{0:T(1024)}, f32[768]{0:T(1024)S(1)}, u32[]{:S(2)}) copy-start(f32[768]{0:T(1024)S(1)} %convert_element_type.149) | copy-start | bytes 9220
  88.3 23.6 %copy-start.6 = (bf16[1024,12,64]{0,2,1:T(8,128)(2,1)S(1)}, bf16[1024,12,64]{0,2,1:T(8,128)(2,1)}, u32[]{:S(2)}) copy-start(bf16[1024,12,64]{0,2,1:T(8,128)(2,1)} %get-tuple-element.535) | copy-start | bytes 4718596 | tf_op jit(solution)/shard_map/while
  99.4 15.8 %copy-start = (f32[12,512,1024]{2,1,0:T(8,128)S(1)}, f32[12,512,1024]{2,1,0:T(8,128)}, u32[]{:S(2)}) copy-start(f32[12,512,1024]{2,1,0:T(8,128)} %get-tuple-element.495) | copy-start | bytes 75497472 | tf_op jit(solution)/shard_map/while
  124.1 23.8 %copy-start.6 = (bf16[1024,12,64]{0,2,1:T(8,128)(2,1)S(1)}, bf16[1024,12,64]{0,2,1:T(8,128)(2,1)}, u32[]{:S(2)}) copy-start(bf16[1024,12,64]{0,2,1:T(8,128)(2,1)} %get-tuple-element.535) | copy-start | bytes 4718596 | tf_op jit(solution)/shard_map/while
  134.8 16.5 %copy-start = (f32[12,512,1024]{2,1,0:T(8,128)S(1)}, f32[12,512,1024]{2,1,0:T(8,128)}, u32[]{:S(2)}) copy-start(f32[12,512,1024]{2,1,0:T(8,128)} %get-tuple-element.495) | copy-start | bytes 75497472 | tf_op jit(solution)/shard_map/while
  169.8 75.0 %copy-start.12 = (f32[1024,768]{0,1:T(8,128)}, f32[1024,768]{0,1:T(8,128)S(1)}, u32[]{:S(2)}) copy-start(f32[1024,768]{0,1:T(8,128)S(1)} %get-tuple-element.378) | copy-start | bytes 9437188
  169.8 75.0 %copy-start.34 = (f32[1024]{0:T(1024)}, f32[1024]{0:T(1024)S(1)}, u32[]{:S(2)}) copy-start(f32[1024]{0:T(1024)S(1)} %broadcast_multiply_fusion) | copy-start | bytes 12292
  170.2 74.6 %copy-start.44 = (f32[1024]{0:T(1024)}, f32[1024]{0:T(1024)S(1)}, u32[]{:S(2)}) copy-start(f32[1024]{0:T(1024)S(1)} %fusion.54) | copy-start | bytes 12292
  257.3 250.1 %reduce-scatter.8.cloned.1.call-start = ((), (), s32[]{:S(2)}) async-start(), calls=%async_computation.9 | async-start | bytes 7962624 | tf_op jit(solution)/shard_map/reduce_scatter | solution.py:249
  258.2 12.3 %copy-start.14 = (bf16[2,512,12,64]{1,3,2,0:T(8,128)(2,1)S(1)}, bf16[2,512,12,64]{1,3,2,0:T(8,128)(2,1)}, u32[]{:S(2)}) copy-start(bf16[2,512,12,64]{1,3,2,0:T(8,128)(2,1)} %get-tuple-element.572) | copy-start | bytes 4718596 | tf_op jit(solution)/shard_map/while
  342.1 11.4 %copy-start.14 = (bf16[2,512,12,64]{1,3,2,0:T(8,128)(2,1)S(1)}, bf16[2,512,12,64]{1,3,2,0:T(8,128)(2,1)}, u32[]{:S(2)}) copy-start(bf16[2,512,12,64]{1,3,2,0:T(8,128)(2,1)} %get-tuple-element.572) | copy-start | bytes 4718596 | tf_op jit(solution)/shard_map/while
  441.4 146.3 %reduce-scatter.12.cloned.1.call-start = ((), (), s32[]{:S(2)}) async-start(), calls=%async_computation.11 | async-start | bytes 10616832 | tf_op jit(solution)/shard_map/reduce_scatter | solution.py:157
  452.9 215.2 %reduce-scatter.14.cloned.1.call-start = ((), (), s32[]{:S(2)}) async-start(), calls=%async_computation.12 | async-start | bytes 10616832 | tf_op jit(solution)/shard_map/reduce_scatter | solution.py:159
  463.6 242.3 %reduce-scatter.16.cloned.1.call-start = ((), (), s32[]{:S(2)}) async-start(), calls=%async_computation.13 | async-start | bytes 442368
  469.6 314.7 %all-reduce.19.cloned.1.call-start = ((), (), s32[]{:S(2)}) async-start(), calls=%async_computation.14 | async-start | bytes 3538944 | tf_op jit(solution)/shard_map/psum | solution.py:257
  469.6 10.6 %copy-start.18 = (bf16[1024,12,64]{0,2,1:T(8,128)(2,1)S(1)}, bf16[1024,12,64]{0,2,1:T(8,128)(2,1)}, u32[]{:S(2)}) copy-start(bf16[1024,12,64]{0,2,1:T(8,128)(2,1)} %copy-done.17) | copy-start | bytes 4718596
  469.6 10.6 %copy-start.20 = (bf16[1024,12,64]{0,2,1:T(8,128)(2,1)S(1)}, bf16[1024,12,64]{0,2,1:T(8,128)(2,1)}, u32[]{:S(2)}) copy-start(bf16[1024,12,64]{0,2,1:T(8,128)(2,1)} %copy-done.19) | copy-start | bytes 4718596
  469.6 10.6 %copy-start.57 = (bf16[768,2304]{1,0:T(8,128)(2,1)S(1)}, bf16[768,2304]{1,0:T(8,128)(2,1)}, u32[]{:S(2)}) copy-start(bf16[768,2304]{1,0:T(8,128)(2,1)} %all-gather.7.cloned.1.call-done) | copy-start | bytes 10616836
  (48 other events, 159.6 us)
Sparse Core Ops, SparseCore 0:
  9.9 36.7 all-gather.6
  48.6 23.9 all-gather.8
  74.5 38.7 all-gather.10
  115.0 38.7 all-gather.12
  257.4 42.6 reduce-scatter.9
  441.5 65.8 reduce-scatter.7
  510.9 76.8 reduce-scatter.11
  591.2 76.8 reduce-scatter.13
  671.1 33.8 reduce-scatter.15
  708.7 75.5 all-reduce.18
where the time goes:
time: 809 us; the launch traced here: 798 us
  matrix products  291 us (36%)
  waiting for transfers between devices  234 us (29%)
  other arithmetic  112 us (14%)
  blocking collectives  78.6 us (10%)
  local copies, waits for them, and re-layouts  64.6 us (8%)
  between operations  17.3 us (2%)
    reduce_scatter x1, waiting for transfers between devices, on_device(): lax.psum_scatter(mlp_terms[2], 'fsdp', scatter_dimension=0, tiled=True)  78.4 us
    reduce_scatter x1, waiting for transfers between devices, on_device(): lax.psum_scatter(mlp_terms[4], 'fsdp', scatter_dimension=0, tiled=True)  78.2 us
    psum x1, waiting for transfers between devices, on_device(): lax.psum(attn_sums[2].astype(jnp.bfloat16), 'dp').astype(jnp.float32)  61.4 us
    unnamed x2, blocking collectives  50 us
    dot_general x4, matrix products, masked_scores(): jnp.einsum('qhd,khd->hqk', query_block, key_rows, preferred_element_type=...  45.4 us
    convert_element_type x2, other arithmetic, attend_back(): grad_scores = (weights * (grad_weights - inner)).astype(jnp.bfloat16)  42.6 us
    dot_general x1, matrix products, on_device(): jnp.dot(hidden_second, up_full, preferred_element_type=jnp.float32)  37.9 us
    dot_general x2, matrix products, attend_back(): jnp.einsum('qhd,khd->hqk', grad_block, value_rows, preferred_element_type...  36.4 us
  transfers between devices with their start and end apart: 10, of which 4 were waited for; matrix products, arithmetic and copies ran while one was open for 50% of the time, Pallas kernels for 0%

commit v1 on v0

--- a/solution.py
+++ b/solution.py
@@ -254,7 +254,9 @@
     totals = (
         lax.psum(attn_sums[0].astype(jnp.bfloat16), "dp").astype(jnp.float32),
         lax.psum(attn_sums[1].astype(jnp.bfloat16), "dp").astype(jnp.float32),
-        lax.psum(attn_sums[2].astype(jnp.bfloat16), "dp").astype(jnp.float32),
+        jnp.sum(lax.all_gather(attn_sums[2].astype(jnp.bfloat16), "dp"), axis=0).astype(
+            jnp.float32
+        ),
         lax.psum(attn_sums[3].astype(jnp.bfloat16), "dp").astype(jnp.float32),
         lax.psum(attn_sums[4].astype(jnp.bfloat16), "dp").astype(jnp.float32),
         lax.psum(attn_sums[5].astype(jnp.bfloat16), "dp").astype(jnp.float32),

time: 809 us -> 885 us (1.094)
  waiting for transfers between devices: 234 us -> 293 us
    reduce_scatter x1, waiting for transfers between devices: 12.8 us -> 33.6 us  [on_device(): lax.psum_scatter(attn_terms[2], 'fsdp', scatter_dimension=0, tiled=True)]
    all_gather x0 -> x1, waiting for transfers between devices: none -> 20.2 us  [on_device(): lax.all_gather(attn_sums[2].astype(jnp.bfloat16), 'dp')]
    reduce_scatter x1, waiting for transfers between devices: 0.01 us -> 18.5 us  [on_device(): lax.psum_scatter(attn_terms[4], 'fsdp', scatter_dimension=0, tiled=True)]
    unnamed x138 -> x118, local copies, waits for them, and re-layouts: 28.8 us -> 30.1 us
  transfers between devices with their start and end apart: 10 -> 11, of which waited for: 4 -> 6; matrix products, arithmetic and copies ran while one was open for 50% -> 27% of each run, Pallas kernels for 0% -> 0%
where the time goes in v1:
time: 885 us; the launch traced here: 874 us
  matrix products  294 us (33%)
  waiting for transfers between devices  293 us (33%)
  other arithmetic  118 us (13%)
  blocking collectives  79.1 us (9%)
  local copies, waits for them, and re-layouts  71.7 us (8%)
  between operations  17 us (2%)
    reduce_scatter x1, waiting for transfers between devices, on_device(): lax.psum_scatter(mlp_terms[2], 'fsdp', scatter_dimension=0, tiled=True)  78.7 us
    reduce_scatter x1, waiting for transfers between devices, on_device(): lax.psum_scatter(mlp_terms[4], 'fsdp', scatter_dimension=0, tiled=True)  78.2 us
    psum x1, waiting for transfers between devices, on_device(): lax.psum(attn_sums[4].astype(jnp.bfloat16), 'dp').astype(jnp.float32)  61.2 us
    unnamed x2, blocking collectives  50.1 us
    dot_general x4, matrix products, masked_scores(): jnp.einsum('qhd,khd->hqk', query_block, key_rows, preferred_element_type=...  44.6 us
    convert_element_type x2, other arithmetic, attend_back(): grad_scores = (weights * (grad_weights - inner)).astype(jnp.bfloat16)  42.4 us
    dot_general x1, matrix products, on_device(): jnp.dot(hidden_second, up_full, preferred_element_type=jnp.float32)  37.8 us
    dot_general x2, matrix products, attend_back(): jnp.einsum('qhd,khd->hqk', grad_block, value_rows, preferred_element_type...  36.1 us
  transfers between devices with their start and end apart: 11, of which 6 were waited for; matrix products, arithmetic and copies ran while one was open for 27% of the time, Pallas kernels for 0%

profile of v1, /device:TPU:0, one launch (start us, length us, event | category | flops | bytes accessed | tf_op | source)
XLA Modules:
  0.0 874.4 jit_solution(17354933475723421737)
XLA Ops:
  17.8 26.7 %all-reduce.14 = (bf16[768]{0:T(1024)(128)(2,1)S(1)}, bf16[768]{0:T(1024)(128)(2,1)S(1)}, bf16[768]{0:T(1024)(128)(2,1)S(1)}, bf16[768]{0:T(1024)(128)(2,1)S(1)}...) all-reduce(bf16[768]{0:T(1024)(128)(2,1)S(1)} %dynamic-update-slice., ...), channel_id=1, replica_groups=mesh['fsdp'=8,'dp'=4] {'fsdp'}, use_global_device_ids=true, to_apply=%add.1 | all-reduce | flops 4608 | bytes 18432
  87.3 72.0 %while.27 = (s32[]{:T(128)}, bf16[2,512,12,64]{1,3,2,0:T(8,128)(2,1)}, f32[2,12,512]{2,1,0:T(8,128)S(1)}, s32[2,512]{1,0:T(2,128)S(1)}, s32[1024]{0:T(1024)S(1)}...) while((s32[]{:T(128)}, ...), condition=%wide.region_5.6_spmd, body=%wide.region_2.5_spmd.sunk | while | flops 1687021568 | bytes 189499568 | solution.py:90
  98.7 12.4 %fusion.115 = f32[12,512]{1,0:T(8,128)S(1)} fusion(f32[12,512,1024]{2,1,0:T(8,128)} %get-tuple-element.494, f32[12,512]{1,0:T(8,128)S(1)} %get-tuple-element.495, pred[512,1024]{1,0:T(8,128)(4,1)S(1)} %broadcast_compare_fusion.4), kind=kLoop, calls=%fused_computation.4.clone.1 | loop fusion | flops 25159680 | bytes 25739264 | tf_op jit(solution)/shard_map/while/body/eval_jaxpr/reduce_sum | solution.py:82
  134.0 13.1 %fusion.115 = f32[12,512]{1,0:T(8,128)S(1)} fusion(f32[12,512,1024]{2,1,0:T(8,128)} %get-tuple-element.494, f32[12,512]{1,0:T(8,128)S(1)} %get-tuple-element.495, pred[512,1024]{1,0:T(8,128)(4,1)S(1)} %broadcast_compare_fusion.4), kind=kLoop, calls=%fused_computation.4.clone.1 | loop fusion | flops 25159680 | bytes 25739264 | tf_op jit(solution)/shard_map/while/body/eval_jaxpr/reduce_sum | solution.py:82
  170.0 37.8 %multiply_convert_fusion.1 = (bf16[1024,3072]{1,0:T(8,128)(2,1)}, f32[1024,3072]{1,0:T(8,128)}, f32[1024,3072]{1,0:T(8,128)}) fusion(f32[3072]{0:T(1024)S(1)} %bitcast.153, bf16[768,3072]{1,0:T(8,128)(2,1)} %all-gather.13.cloned.1.call-done, f32[1024,768]{0,1:T(8,128)} %copy-done.9, f32[768]{0:T(1024)S(1)} %copy-done.42, f32[768]{0:T(1024)S(1)} %copy-done.33, ...), kind=kOutput, calls=%fused_computation.50 | convolution fusion | flops 5043388416 | bytes 39348224 | tf_op jit(solution)/shard_map/dot_general | solution.py:109
  207.8 18.9 %convert_reduce_fusion = (f32[3072]{0:T(1024)}, bf16[1024,3072]{1,0:T(8,128)(2,1)}) fusion(f32[1024,3072]{1,0:T(8,128)} %get-tuple-element.364, bf16[1024,768]{1,0:T(8,128)(2,1)} %param.33, bf16[3072,768]{1,0:T(8,128)(2,1)} %all-gather.15.cloned.1.call-done, f32[1024,3072]{1,0:T(8,128)} %get-tuple-element.378, f32[3072]{0:T(1024)S(1)} %bitcast.154), kind=kOutput, calls=%fused_computation.48 | convolution fusion | flops 4885312512 | bytes 37773312 | tf_op jit(solution)/shard_map/td,fd->tf/dot_general | solution.py:134
  261.0 170.0 %while.28 = (s32[]{:T(128)}, f32[1024,12,64]{0,2,1:T(8,128)}, f32[1024,12,64]{0,2,1:T(8,128)}, bf16[2,512,12,64]{1,3,2,0:T(8,128)(2,1)}, bf16[2,512,12,64]{1,3,2...) while((s32[]{:T(128)}, f32[1024,12,64]{0,2,1:T(8,128)}, ...), condition=%wide.region_12.13_spmd.clone, body=%wide.region_10.12_spmd.clone.sunk | while | flops 4125747200 | bytes 231926000 | solution.py:210
  262.9 11.5 %fusion.126 = f32[12,512,1024]{2,1,0:T(8,128)} fusion(bf16[1024,12,64]{0,2,1:T(8,128)(2,1)S(1)} %get-tuple-element.569, bf16[2,512,12,64]{1,3,2,0:T(8,128)(2,1)} %copy-done.2, s32[]{:T(128)S(6)} %copy.130), kind=kOutput, calls=%fused_computation.32.clone.1 | convolution fusion | flops 805306368 | bytes 27525124 | tf_op jit(solution)/shard_map/while/body/eval_jaxpr/qhd,khd->hqk/dot_general | solution.py:71
  274.3 13.4 %bitcast_add_fusion.5 = f32[1024,12,64]{0,2,1:T(8,128)} fusion(f32[1024,12,64]{0,2,1:T(8,128)} %get-tuple-element.551, f32[12,512,1024]{2,1,0:T(8,128)} %fusion.126, f32[12,512]{1,0:T(8,128)S(1)} %dynamic-slice_bitcast_fusion.2, pred[512,1024]{1,0:T(8,128)(4,1)S(1)} %broadcast_compare_fusion.5, pred[]{:T(512)S(6)} %compare.3, ...), kind=kOutput, calls=%fused_computation.24.clone.1 | convolution fusion | flops 832045056 | bytes 32800772 | tf_op jit(solution)/shard_map/while/body/eval_jaxpr/hqk,qhd->khd/dot_general | solution.py:188
  287.8 18.1 %multiply_reduce_fusion.5 = (f32[12,512]{1,0:T(8,128)S(1)}, f32[12,512,1024]{2,1,0:T(8,128)}) fusion(f32[12,512,1024]{2,1,0:T(8,128)} %fusion.126, f32[12,512]{1,0:T(8,128)S(1)} %dynamic-slice_bitcast_fusion.2, pred[512,1024]{1,0:T(8,128)(4,1)S(1)} %broadcast_compare_fusion.5, bf16[1024,12,64]{0,2,1:T(8,128)(2,1)} %get-tuple-element.572, ...), kind=kOutput, calls=%fused_computation.19.clone.1 | convolution fusion | flops 836757504 | bytes 53264388 | tf_op jit(solution)/shard_map/while/body/eval_jaxpr/qhd,khd->hqk/dot_general | solution.py:191
  305.8 21.2 %multiply_convert_fusion.3 = bf16[12,512,1024]{2,1,0:T(8,128)(2,1)} fusion(f32[12,512,1024]{2,1,0:T(8,128)} %get-tuple-element.507, f32[12,512,1024]{2,1,0:T(8,128)} %fusion.126, f32[12,512]{1,0:T(8,128)S(1)} %get-tuple-element.508, f32[12,512]{1,0:T(8,128)S(1)} %dynamic-slice_bitcast_fusion.2, pred[512,1024]{1,0:T(8,128)(4,1)S(1)} %broadcast_compare_fusion.5), kind=kLoop, calls=%fused_computation.18.clone.1 | loop fusion | flops 37748736 | bytes 63488000 | tf_op jit(solution)/shard_map/while/body/eval_jaxpr/convert_element_type | solution.py:195
  346.7 11.5 %fusion.126 = f32[12,512,1024]{2,1,0:T(8,128)} fusion(bf16[1024,12,64]{0,2,1:T(8,128)(2,1)S(1)} %get-tuple-element.569, bf16[2,512,12,64]{1,3,2,0:T(8,128)(2,1)} %copy-done.2, s32[]{:T(128)S(6)} %copy.130), kind=kOutput, calls=%fused_computation.32.clone.1 | convolution fusion | flops 805306368 | bytes 27525124 | tf_op jit(solution)/shard_map/while/body/eval_jaxpr/qhd,khd->hqk/dot_general | solution.py:71
  358.2 14.3 %bitcast_add_fusion.5 = f32[1024,12,64]{0,2,1:T(8,128)} fusion(f32[1024,12,64]{0,2,1:T(8,128)} %get-tuple-element.551, f32[12,512,1024]{2,1,0:T(8,128)} %fusion.126, f32[12,512]{1,0:T(8,128)S(1)} %dynamic-slice_bitcast_fusion.2, pred[512,1024]{1,0:T(8,128)(4,1)S(1)} %broadcast_compare_fusion.5, pred[]{:T(512)S(6)} %compare.3, ...), kind=kOutput, calls=%fused_computation.24.clone.1 | convolution fusion | flops 832045056 | bytes 32800772 | tf_op jit(solution)/shard_map/while/body/eval_jaxpr/hqk,qhd->khd/dot_general | solution.py:188
  372.5 18.1 %multiply_reduce_fusion.5 = (f32[12,512]{1,0:T(8,128)S(1)}, f32[12,512,1024]{2,1,0:T(8,128)}) fusion(f32[12,512,1024]{2,1,0:T(8,128)} %fusion.126, f32[12,512]{1,0:T(8,128)S(1)} %dynamic-slice_bitcast_fusion.2, pred[512,1024]{1,0:T(8,128)(4,1)S(1)} %broadcast_compare_fusion.5, bf16[1024,12,64]{0,2,1:T(8,128)(2,1)} %get-tuple-element.572, ...), kind=kOutput, calls=%fused_computation.19.clone.1 | convolution fusion | flops 836757504 | bytes 53264388 | tf_op jit(solution)/shard_map/while/body/eval_jaxpr/qhd,khd->hqk/dot_general | solution.py:191
  390.6 21.2 %multiply_convert_fusion.3 = bf16[12,512,1024]{2,1,0:T(8,128)(2,1)} fusion(f32[12,512,1024]{2,1,0:T(8,128)} %get-tuple-element.507, f32[12,512,1024]{2,1,0:T(8,128)} %fusion.126, f32[12,512]{1,0:T(8,128)S(1)} %get-tuple-element.508, f32[12,512]{1,0:T(8,128)S(1)} %dynamic-slice_bitcast_fusion.2, pred[512,1024]{1,0:T(8,128)(4,1)S(1)} %broadcast_compare_fusion.5), kind=kLoop, calls=%fused_computation.18.clone.1 | loop fusion | flops 37748736 | bytes 63488000 | tf_op jit(solution)/shard_map/while/body/eval_jaxpr/convert_element_type | solution.py:195
  450.7 11.2 %fusion.60 = f32[768,3072]{1,0:T(8,128)} fusion(bf16[1024,3072]{1,0:T(8,128)(2,1)} %get-tuple-element.384, f32[1024,768]{0,1:T(8,128)} %copy-done.9, f32[768]{0:T(1024)S(1)} %copy-done.43, f32[768]{0:T(1024)S(1)} %copy-done.34, f32[1024]{0:T(1024)S(1)} %copy-done.36, f32[1024]{0:T(1024)S(1)} %copy-done.26), kind=kOutput, calls=%fused_computation.121 | convolution fusion | flops 4835770368 | bytes 18888704 | tf_op jit(solution)/shard_map/td,tf->df/dot_general | solution.py:138
  478.3 33.6 %reduce-scatter.8.cloned.1.call-done = f32[96,2304]{1,0:T(8,128)} async-done(((f32[768,2304]{1,0:T(8,128)}), f32[96,2304]{1,0:T(8,128)}) %reduce-scatter.8.cloned.1.call-update) | async-done | bytes 884752 | tf_op jit(solution)/shard_map/reduce_scatter | solution.py:249
  539.0 18.5 %reduce-scatter.10.cloned.1.call-done = f32[96,768]{1,0:T(8,128)} async-done(((f32[768,768]{1,0:T(8,128)}), f32[96,768]{1,0:T(8,128)}) %reduce-scatter.10.cloned.1.call-update) | async-done | bytes 294928 | tf_op jit(solution)/shard_map/reduce_scatter | solution.py:251
  559.1 78.7 %reduce-scatter.12.cloned.1.call-done = f32[96,3072]{1,0:T(8,128)} async-done(((f32[768,3072]{1,0:T(8,128)}), f32[96,3072]{1,0:T(8,128)}) %reduce-scatter.12.cloned.1.call-update) | async-done | bytes 1179664 | tf_op jit(solution)/shard_map/reduce_scatter | solution.py:157
  640.0 78.2 %reduce-scatter.14.cloned.1.call-done = f32[384,768]{1,0:T(8,128)} async-done(((f32[3072,768]{1,0:T(8,128)}), f32[384,768]{1,0:T(8,128)}) %reduce-scatter.14.cloned.1.call-update) | async-done | bytes 1179664 | tf_op jit(solution)/shard_map/reduce_scatter | solution.py:159
  732.5 23.4 %all-reduce.13 = (bf16[768]{0:T(1024)(128)(2,1)S(1)}, bf16[768]{0:T(1024)(128)(2,1)S(1)}, bf16[768]{0:T(1024)(128)(2,1)S(1)}, bf16[768]{0:T(1024)(128)(2,1)S(1)}...) all-reduce(f32[768]{0:T(1024)S(1)} %get-tuple-element.293, ...), channel_id=3, replica_groups=mesh['fsdp'=8,'dp'=4] {'fsdp'}, use_global_device_ids=true, to_apply=%region_16.17.clone | all-reduce | flops 7680 | bytes 46080
  760.8 12.4 %all-reduce.15 = (bf16[96]{0:T(256)(128)(2,1)S(1)}, bf16[96]{0:T(256)(128)(2,1)S(1)}, bf16[2,96]{1,0:T(2,128)(2,1)S(1)}, bf16[96]{0:T(256)(128)(2,1)S(1)}, bf16[...) all-reduce(bf16[96]{0:T(256)(128)(2,1)S(1)} %dynamic-slice.33, ...), channel_id=1, replica_groups=mesh['fsdp'=8,'dp'=4] {'dp'}, use_global_device_ids=true, to_apply=%region_17.18 | all-reduce | flops 1152 | bytes 4608 | tf_op jit(solution)/shard_map/psum | solution.py:255
  777.4 20.2 %all-gather.17.cloned.1.call-done = bf16[384,2304]{1,0:T(8,128)(2,1)} async-done(((bf16[96,2304]{1,0:T(8,128)(2,1)}), bf16[384,2304]{1,0:T(8,128)(2,1)}) %all-gather.17.cloned.1.call-update) | async-done | bytes 1769488 | tf_op jit(solution)/shard_map/all_gather | solution.py:257
  800.4 61.2 %all-reduce.19.cloned.1.call-done = (bf16[96,768]{1,0:T(8,128)(2,1)}, bf16[96,3072]{1,0:T(8,128)(2,1)}, bf16[384,768]{1,0:T(8,128)(2,1)}) async-done(((bf16[96,768]{1,0:T(8,128)(2,1)}, bf16[96,3072]{1,0:T(8,128)(2,1)}, bf16[384,768]{1,0:T(8,128)(2,1)}), (bf16[96,768]{1,0:T(8,128)(2,1)}, bf16[96,3072]{1,0:T(8,128)(2,1)}, bf16[384,768]{1,0:T(8,128)(2,1)})) %all-reduce.19.cloned.1.call-update) | async-done | bytes 1327120 | tf_op jit(solution)/shard_map/psum | solution.py:261
  (267 shorter events, 280.8 us)
Async XLA Ops:
  7.2 61.5 %all-gather.9.cloned.1.call-start = ((), (), s32[]{:S(2)}) async-start(), calls=%async_computation.5 | async-start | bytes 3981312 | tf_op jit(solution)/shard_map/all_gather | solution.py:45
  7.9 156.1 %all-gather.11.cloned.1.call-start = ((), (), s32[]{:S(2)}) async-start(), calls=%async_computation.6 | async-start | bytes 1327104 | tf_op jit(solution)/shard_map/all_gather | solution.py:47
  8.7 161.3 %all-gather.13.cloned.1.call-start = ((), (), s32[]{:S(2)}) async-start(), calls=%async_computation.7 | async-start | bytes 5308416 | tf_op jit(solution)/shard_map/all_gather | solution.py:99
  9.4 198.4 %all-gather.15.cloned.1.call-start = ((), (), s32[]{:S(2)}) async-start(), calls=%async_computation.8 | async-start | bytes 5308416 | tf_op jit(solution)/shard_map/all_gather | solution.py:101
  10.0 501.9 %reduce-scatter.8.cloned.1.call-start = ((), (), s32[]{:S(2)}) async-start(), calls=%async_computation.9 | async-start | bytes 7962624 | tf_op jit(solution)/shard_map/reduce_scatter | solution.py:249
  44.5 24.3 %copy-start.44 = (f32[768]{0:T(1024)}, f32[768]{0:T(1024)S(1)}, u32[]{:S(2)}) copy-start(f32[768]{0:T(1024)S(1)} %convert_element_type.152) | copy-start | bytes 9220
  44.5 24.3 %copy-start.23 = (f32[768]{0:T(1024)}, f32[768]{0:T(1024)S(1)}, u32[]{:S(2)}) copy-start(f32[768]{0:T(1024)S(1)} %convert_element_type.151) | copy-start | bytes 9220
  87.7 23.5 %copy-start.4 = (bf16[1024,12,64]{0,2,1:T(8,128)(2,1)S(1)}, bf16[1024,12,64]{0,2,1:T(8,128)(2,1)}, u32[]{:S(2)}) copy-start(bf16[1024,12,64]{0,2,1:T(8,128)(2,1)} %get-tuple-element.534) | copy-start | bytes 4718596 | tf_op jit(solution)/shard_map/while
  98.7 15.8 %copy-start = (f32[12,512,1024]{2,1,0:T(8,128)S(1)}, f32[12,512,1024]{2,1,0:T(8,128)}, u32[]{:S(2)}) copy-start(f32[12,512,1024]{2,1,0:T(8,128)} %get-tuple-element.494) | copy-start | bytes 75497472 | tf_op jit(solution)/shard_map/while
  123.4 23.7 %copy-start.4 = (bf16[1024,12,64]{0,2,1:T(8,128)(2,1)S(1)}, bf16[1024,12,64]{0,2,1:T(8,128)(2,1)}, u32[]{:S(2)}) copy-start(bf16[1024,12,64]{0,2,1:T(8,128)(2,1)} %get-tuple-element.534) | copy-start | bytes 4718596 | tf_op jit(solution)/shard_map/while
  134.0 16.4 %copy-start = (f32[12,512,1024]{2,1,0:T(8,128)S(1)}, f32[12,512,1024]{2,1,0:T(8,128)}, u32[]{:S(2)}) copy-start(f32[12,512,1024]{2,1,0:T(8,128)} %get-tuple-element.494) | copy-start | bytes 75497472 | tf_op jit(solution)/shard_map/while
  168.0 77.2 %copy-start.25 = (f32[1024]{0:T(1024)}, f32[1024]{0:T(1024)S(1)}, u32[]{:S(2)}) copy-start(f32[1024]{0:T(1024)S(1)} %broadcast_multiply_fusion) | copy-start | bytes 12292
  170.0 75.1 %copy-start.35 = (f32[1024]{0:T(1024)}, f32[1024]{0:T(1024)S(1)}, u32[]{:S(2)}) copy-start(f32[1024]{0:T(1024)S(1)} %fusion.54) | copy-start | bytes 12292
  262.9 11.5 %copy-start.13 = (bf16[2,512,12,64]{1,3,2,0:T(8,128)(2,1)S(1)}, bf16[2,512,12,64]{1,3,2,0:T(8,128)(2,1)}, u32[]{:S(2)}) copy-start(bf16[2,512,12,64]{1,3,2,0:T(8,128)(2,1)} %get-tuple-element.571) | copy-start | bytes 4718596 | tf_op jit(solution)/shard_map/while
  327.1 9.5 %copy-start.3 = (bf16[2,512,12,64]{1,3,2,0:T(8,128)(2,1)S(1)}, bf16[2,512,12,64]{1,3,2,0:T(8,128)(2,1)}, u32[]{:S(2)}) copy-start(bf16[2,512,12,64]{1,3,2,0:T(8,128)(2,1)} %copy-done.2) | copy-start | bytes 4718596 | tf_op jit(solution)/shard_map/while
  346.7 11.5 %copy-start.13 = (bf16[2,512,12,64]{1,3,2,0:T(8,128)(2,1)S(1)}, bf16[2,512,12,64]{1,3,2,0:T(8,128)(2,1)}, u32[]{:S(2)}) copy-start(bf16[2,512,12,64]{1,3,2,0:T(8,128)(2,1)} %get-tuple-element.571) | copy-start | bytes 4718596 | tf_op jit(solution)/shard_map/while
  411.8 9.5 %copy-start.3 = (bf16[2,512,12,64]{1,3,2,0:T(8,128)(2,1)S(1)}, bf16[2,512,12,64]{1,3,2,0:T(8,128)(2,1)}, u32[]{:S(2)}) copy-start(bf16[2,512,12,64]{1,3,2,0:T(8,128)(2,1)} %copy-done.2) | copy-start | bytes 4718596 | tf_op jit(solution)/shard_map/while
  445.8 111.7 %reduce-scatter.10.cloned.1.call-start = ((), (), s32[]{:S(2)}) async-start(), calls=%async_computation.10 | async-start | bytes 2654208 | tf_op jit(solution)/shard_map/reduce_scatter | solution.py:251
  450.6 187.2 %reduce-scatter.12.cloned.1.call-start = ((), (), s32[]{:S(2)}) async-start(), calls=%async_computation.11 | async-start | bytes 10616832 | tf_op jit(solution)/shard_map/reduce_scatter | solution.py:157
  462.0 256.2 %reduce-scatter.14.cloned.1.call-start = ((), (), s32[]{:S(2)}) async-start(), calls=%async_computation.12 | async-start | bytes 10616832 | tf_op jit(solution)/shard_map/reduce_scatter | solution.py:159
  472.6 287.4 %reduce-scatter.16.cloned.1.call-start = ((), (), s32[]{:S(2)}) async-start(), calls=%async_computation.14 | async-start | bytes 442368
  477.0 320.6 %all-gather.17.cloned.1.call-start = ((), (), s32[]{:S(2)}) async-start(), calls=%async_computation.13 | async-start | bytes 2211840 | tf_op jit(solution)/shard_map/all_gather | solution.py:257
  513.9 347.6 %all-reduce.19.cloned.1.call-start = ((), (), s32[]{:S(2)}) async-start(), calls=%async_computation.15 | async-start | bytes 2654208 | tf_op jit(solution)/shard_map/psum | solution.py:261
  539.0 181.4 %copy-start.32 = (f32[1024]{0:T(1024)S(1)}, f32[1024]{0:T(1024)}, u32[]{:S(2)}) copy-start(f32[1024]{0:T(1024)} %copy-done.31) | copy-start | bytes 12292
  (41 other events, 151.6 us)
Sparse Core Ops, SparseCore 0:
  9.9 36.7 all-gather.8
  48.6 23.9 all-gather.10
  74.5 38.7 all-gather.12
  115.0 38.8 all-gather.14
  445.9 65.9 reduce-scatter.7
  515.1 42.3 reduce-scatter.9
  561.0 76.7 reduce-scatter.11
  641.3 76.8 reduce-scatter.13
  721.3 33.9 reduce-scatter.15
  757.3 40.2 all-gather.16
  801.3 60.1 all-reduce.18
